TPU v7x, 256 devices: a whole 4x4x8 slice. The times are simulated.
256 devices in a mesh: band: 16 (over y, x_lo, core), grid: 16 (over z, x_hi).
Axes of the slice: x: 4 (x_hi: 2, x_lo: 2; x = x_hi * 2 + x_lo), y: 4, z: 8, core: 2. Of those that a mesh axis runs over, the one named last changes fastest.
Arguments:
- own_orbitals: bfloat16 [32, 128, 128, 128], P('band', 'grid'), may hold values from -9 to 9
- resident_orbitals: bfloat16 [32, 128, 128, 128], P('band', 'grid'), may hold values from -9 to 9
- pair_lists: int32 [16, 2, 2, 2], P('band'), may hold values from 0 to 1, as said below
- pair_counts: int32 [16, 2], P('band'), may hold values from 1 to 2, as said below
Outputs:
- exchange_block: bfloat16 [32, 128, 128, 128], P('band', 'grid')
- intersection: float32 [32, 2], P('band')
Inputs may be any that keep to these rules, and one draw needn't show every extreme that they name: pair_lists[b, l, s] = (i, j) pairs band i of block b with band j of the partner block of list l; the 2 pairs of one list are distinct; slots s >= pair_counts[b, l] hold pairs that are not used. `pair_counts`: in each of the two lists exactly one block has 2 live slots, every other block exactly 1.
All inputs are finite; a program needn't handle non-finite values.
Results may differ from a plain program's by a relative error of at most 0.00045.
Values may be sent and summed in bfloat16 or wider, within the bound.
No kernel may reach another device: no remote copies, remote signals or barrier semaphores. Data moves between devices by JAX's collectives and lax.ppermute only.
A program may use at most 64 MiB of HBM per device.

v0:
```python
import functools
import math

import jax
import jax.numpy as jnp
import numpy as np
from jax import lax
from jax.experimental import pallas as pl
from jax.experimental.pallas import tpu as pltpu
from jax.sharding import PartitionSpec as P

BF16 = jnp.bfloat16
F32 = jnp.float32
TOP = 32760.0
STEPS = 256.0
FLOOR = 2.0**-110
GROUP = 4
OUT_SHARE = 4
BACK_SHARE = 2
LIMIT = pltpu.CompilerParams(vmem_limit_bytes=20 << 20)


def passed_along(x, axis, by):
    length = lax.axis_size(axis)
    return lax.ppermute(x, axis, [(i, (i + by) % length) for i in range(length)])


def cas_halves(length):
    indices = np.arange(length)
    angles = (indices[:, None] * indices[None, :] % length) * (2.0 * math.pi / length)
    table = (np.cos(angles) + np.sin(angles)) / math.sqrt(length)
    high = table.astype(np.float32).astype(BF16)
    low = (table - high.astype(np.float64)).astype(np.float32).astype(BF16)
    return high, low


def right_table(length):
    high, low = cas_halves(length)
    row = np.concatenate([high, low], axis=1)
    return np.concatenate([row, row], axis=0)


def left_table(length):
    high, low = cas_halves(length)
    column = np.concatenate([high, low], axis=0)
    return np.concatenate([column, column], axis=1)


def halves(x):
    high = x.astype(BF16)
    return high, (x - high.astype(F32)).astype(BF16)


def from_right(x, table):
    half = x.shape[1]
    both = jnp.dot(jnp.concatenate(halves(x), axis=1), table, preferred_element_type=F32)
    return both[:, :half] + both[:, half:]


def from_left(x, table):
    half = x.shape[0]
    both = jnp.dot(table, jnp.concatenate(halves(x), axis=0), preferred_element_type=F32)
    return both[:half] + both[half:]


def scale_code(peak):
    return jnp.ceil(jnp.log2(jnp.maximum(peak, FLOOR)) * STEPS)


def decoded_scale(code):
    return jnp.exp2(code * (1.0 / STEPS)) * (1.0 / TOP)


def lane_group(shape, share):
    return lax.broadcasted_iota(jnp.int32, shape, 1) // (shape[1] // share)


def over_lanes(x, share, combine):
    step = x.shape[1]
    while share > 1:
        step, share = step // 2, share // 2
        x = combine(x, pltpu.roll(x, step, 1))
    return x


def packed_codes(codes, share):
    tiles = []
    for start in range(0, len(codes), share):
        tile = codes[start]
        group = lane_group(tile.shape, share)
        for offset, code in enumerate(codes[start + 1 : start + share]):
            tile = jnp.where(group == offset + 1, code, tile)
        tiles.append(tile)
    return tiles


def unpacked_scale(tile, place, share):
    group = lane_group(tile.shape, share)
    return decoded_scale(over_lanes(jnp.where(group == place, tile, 0.0), share, jnp.add))


def encode(load, store, planes, carry, share):
    values = [load(plane) for plane in range(planes)]
    peak = functools.reduce(jnp.maximum, [jnp.abs(value) for value in values])
    code = scale_code(over_lanes(peak, share, jnp.maximum))
    inverse = jnp.exp2(code * (-1.0 / STEPS)) * TOP
    left = None
    for plane, value in enumerate(values):
        scaled = value * inverse
        if left is not None:
            scaled = scaled + left
        whole = jnp.round(scaled)
        if carry:
            left = scaled - whole
        store(plane, whole.astype(jnp.int32))
    return code


def store_coded(out_ref, piece, first):
    rows = out_ref.shape[2]

    def store(plane, value):
        count = value.shape[0] // rows
        value = value.reshape(count, rows, value.shape[1]).astype(jnp.int16)
        out_ref[pl.ds(piece, count), first + plane] = value

    return store


def store_tile(out_ref, number, tile):
    pieces, _, rows, length = out_ref.shape
    out_ref[:, number] = tile.astype(jnp.int32).reshape(pieces, rows, length).astype(jnp.int16)


def load_tile(got_ref, number):
    pieces, _, rows, length = got_ref.shape
    return got_ref[:, number].astype(jnp.int32).astype(F32).reshape(pieces * rows, length)


def forward_slot(own_ref, first, partner_ref, second, right_ref, left_ref, out_ref, start, field, code_ref):
    planes, length = own_ref.shape[1], own_ref.shape[2]
    pieces, rows = out_ref.shape[0], out_ref.shape[2]
    for pair in range(planes // 2):
        densities = [
            own_ref[first, plane].astype(F32) * partner_ref[second, plane].astype(F32)
            for plane in (pair * 2, pair * 2 + 1)
        ]
        lines = from_right(jnp.concatenate(densities, axis=0), right_ref[...])
        lines = jnp.concatenate([lines[:length], lines[length:]], axis=1)
        lines = from_left(lines, left_ref[...])
        for side in range(2):
            field[pair * 2 + side] = lines[:, side * length : (side + 1) * length]
    for piece in range(0, pieces, GROUP):
        code_ref[pl.ds(piece * rows, GROUP * rows), :] = encode(
            lambda plane: field[plane, pl.ds(piece * rows, GROUP * rows), :],
            store_coded(out_ref, piece, start),
            planes,
            True,
            OUT_SHARE,
        )


def early_kernel(
    lists_ref,
    counts_ref,
    own_hbm,
    resident_hbm,
    right_ref,
    left_ref,
    out_ref,
    kernel_ref,
    codes_ref,
    index_ref,
    field,
    own_ref,
    resident_ref,
    sems,
):
    rows, length = out_ref.shape[2], out_ref.shape[3]
    slots, planes = codes_ref.shape[0], own_ref.shape[1]
    copies = []
    for number, (source, target) in enumerate(((own_hbm, own_ref), (resident_hbm, resident_ref))):
        copy = pltpu.make_async_copy(source, target, sems.at[number])
        copy.start()
        copies.append(copy)
    index_ref[0] = counts_ref[0, 0] + counts_ref[0, 1] - 2
    place = lax.axis_index("grid")
    first = lax.broadcasted_iota(jnp.int32, (length, length), 0)
    last = lax.broadcasted_iota(jnp.int32, (length, length), 1)
    first = jnp.minimum(first, length - first).astype(F32)
    last = jnp.minimum(last, length - last).astype(F32)
    around = first * first + last * last
    for row in range(rows):
        middle = place * rows + row
        middle = jnp.minimum(middle, length - middle).astype(F32)
        squared = around + middle * middle
        kernel_ref[:, row * length : (row + 1) * length] = jnp.where(
            squared > 0.5, 0.25 * length**1.5 / jnp.maximum(squared, 1.0), 0.0
        )
    for copy in copies:
        copy.wait()

    def transform(slot):
        forward_slot(
            own_ref,
            lists_ref[0, 0, slot, 0],
            resident_ref,
            lists_ref[0, 0, slot, 1],
            right_ref,
            left_ref,
            out_ref,
            slot * planes,
            field,
            codes_ref.at[slot],
        )

    transform(0)
    for slot in range(1, slots):

        @pl.when(slot < counts_ref[0, 0])
        def _():
            transform(slot)


def late_kernel(
    slots,
    lists_ref,
    counts_ref,
    own_ref,
    received_ref,
    early_ref,
    early_codes_ref,
    right_ref,
    left_ref,
    out_ref,
    fields,
    codes,
):
    planes = own_ref.shape[1]

    def transform(number, slot):
        forward_slot(
            own_ref,
            lists_ref[0, 1, number, 0],
            received_ref,
            lists_ref[0, 1, number, 1],
            right_ref,
            left_ref,
            out_ref,
            slot * planes,
            fields.at[number],
            codes.at[slot],
        )

    def take(number, slot):
        out_ref[:, slot * planes : (slot + 1) * planes] = early_ref[
            :, number * planes : (number + 1) * planes
        ]
        codes[slot] = early_codes_ref[number]

    take(0, 0)
    if slots == 3:

        @pl.when(counts_ref[0, 0] == 2)
        def _():
            take(1, 2)
            transform(0, 1)

        @pl.when(counts_ref[0, 0] != 2)
        def _():
            transform(0, 1)
            transform(1, 2)

    else:
        transform(0, 1)
    if slots == 4:
        take(1, 2)
        transform(1, 3)
    for number, tile in enumerate(packed_codes([codes[slot] for slot in range(slots)], OUT_SHARE)):
        store_tile(out_ref, slots * planes + number, tile)


def middle_kernel(slots, planes, got_ref, kernel_ref, left_ref, out_ref, before, after, codes):
    pieces, rows = got_ref.shape[0], got_ref.shape[2]
    length = pieces * planes
    for slot in range(slots):
        tile = load_tile(got_ref, slots * planes + slot // OUT_SHARE)
        codes[slot] = unpacked_scale(tile, slot % OUT_SHARE, OUT_SHARE)
    for slot in range(slots):
        for piece in range(pieces):
            scale = codes[slot, pl.ds(piece * rows, rows), :]
            for plane in range(planes):
                start = (piece * planes + plane) * rows
                before[slot, pl.ds(start, rows), :] = (
                    got_ref[piece, slot * planes + plane].astype(jnp.int32).astype(F32) * scale
                )
        for pair in range(rows // 2):
            lines = jnp.concatenate(
                [before[slot, pl.ds(pair * 2 + side, length, stride=rows), :] for side in range(2)],
                axis=1,
            )
            lines = from_left(lines, left_ref[...])
            lines = lines * kernel_ref[:, pair * 2 * length : (pair + 1) * 2 * length]
            lines = from_left(lines, left_ref[...])
            for side in range(2):
                after[slot, pl.ds(pair * 2 + side, length, stride=rows), :] = lines[
                    :, side * length : (side + 1) * length
                ]
        for piece in range(pieces):
            codes[slot, pl.ds(piece * rows, rows), :] = encode(
                lambda plane: after[slot, pl.ds((piece * planes + plane) * rows, rows), :],
                store_coded(out_ref, piece, slot * planes),
                planes,
                False,
                BACK_SHARE,
            )
    for number, tile in enumerate(packed_codes([codes[slot] for slot in range(slots)], BACK_SHARE)):
        store_tile(out_ref, slots * planes + number, tile)


def slot_table(lists_ref, counts_ref, slots):
    table = []
    for slot in range(slots):
        if slot < 2:
            which, place = slot, 0
        elif slots == 3:
            which, place = jnp.where(counts_ref[0, 0] == 2, 0, 1), 1
        else:
            which, place = slot - 2, 1
        table.append((which, lists_ref[0, which, place, 0], lists_ref[0, which, place, 1]))
    return table


def partner_plane(resident_ref, received_ref, which, band, plane):
    if isinstance(which, int):
        chosen = received_ref if which else resident_ref
        return chosen[band, plane].astype(F32)
    return jnp.where(
        which == 1, received_ref[band, plane].astype(F32), resident_ref[band, plane].astype(F32)
    )


def final_kernel(
    slots,
    lists_ref,
    counts_ref,
    own_ref,
    resident_ref,
    received_ref,
    got_ref,
    right_ref,
    left_ref,
    out_hbm,
    terms_ref,
    scales,
    sums,
    out_ref,
    sems,
):
    table = slot_table(lists_ref, counts_ref, slots)
    bands, planes, length = own_ref.shape[:3]
    for slot in range(slots):
        tile = load_tile(got_ref, slots * planes + slot // BACK_SHARE)
        scales[slot] = unpacked_scale(tile, slot % BACK_SHARE, BACK_SHARE)
    sums[...] = jnp.zeros_like(sums)

    def copies(pair):
        return [
            pltpu.make_async_copy(
                out_ref.at[band, pl.ds(pair * 2, 2)],
                out_hbm.at[band, pl.ds(pair * 2, 2)],
                sems.at[pair, band],
            )
            for band in range(bands)
        ]

    for pair in range(planes // 2):
        totals = [[jnp.zeros((length, length), F32) for _ in range(bands)] for _ in range(2)]
        for slot, (which, first, second) in enumerate(table):
            lines = []
            for side in range(2):
                value = load_tile(got_ref, slot * planes + pair * 2 + side)
                lines.append(value * scales[slot])
            lines = from_left(jnp.concatenate(lines, axis=1), left_ref[...])
            lines = jnp.concatenate([lines[:, :length], lines[:, length:]], axis=0)
            lines = from_right(lines, right_ref[...])
            for side in range(2):
                plane = pair * 2 + side
                term = lines[side * length : (side + 1) * length] * partner_plane(
                    resident_ref, received_ref, which, second, plane
                )
                for band in range(bands):
                    totals[side][band] += jnp.where(first == band, term, 0.0)
        for side in range(2):
            plane = pair * 2 + side
            for band in range(bands):
                out_ref[band, plane] = totals[side][band].astype(out_ref.dtype)
                for other in range(bands):
                    product = own_ref[other, plane].astype(F32) * totals[side][band]
                    sums[other * bands + band] += product.reshape(length // 8, 8, length).sum(axis=0)
        if pair:
            for copy in copies(pair - 1):
                copy.start()

    for entry in range(bands * bands):
        row = jnp.sum(sums[entry], axis=0, keepdims=True)
        terms_ref[:, entry // bands, entry % bands : entry % bands + 1, :] = jnp.broadcast_to(
            row[None], (terms_ref.shape[0], 1, row.shape[1])
        )
    for copy in copies(planes // 2 - 1):
        copy.start()
    for pair in range(planes // 2):
        for copy in copies(pair):
            copy.wait()


VMEM = pl.BlockSpec(memory_space=pltpu.VMEM)
SMEM = pl.BlockSpec(memory_space=pltpu.SMEM)
ANY = pl.BlockSpec(memory_space=pl.ANY)


def on_device(right, left, own_orbitals, resident_orbitals, pair_lists, pair_counts):
    bands, planes, length = own_orbitals.shape[:3]
    pieces = lax.axis_size("grid")
    rows = length // pieces
    received = passed_along(resident_orbitals, "band", 1)
    lists, counts = pair_lists, pair_counts
    field = pltpu.VMEM((planes, length, length), F32)

    table = pltpu.VMEM((4, length, length), F32)

    def coded(slots, share):
        tiles = slots * planes + (-(-slots // share) if share else 0)
        return jax.ShapeDtypeStruct((pieces, tiles, rows, length), jnp.int16)

    early, kernel, codes, index = pl.pallas_call(
        early_kernel,
        out_shape=(
            coded(2, 0),
            jax.ShapeDtypeStruct((length, rows * length), F32),
            jax.ShapeDtypeStruct((2, length, length), F32),
            jax.ShapeDtypeStruct((1,), jnp.int32),
        ),
        in_specs=[SMEM, SMEM, ANY, ANY, VMEM, VMEM],
        out_specs=(VMEM, VMEM, VMEM, SMEM),
        scratch_shapes=[
            field,
            pltpu.VMEM(own_orbitals.shape, BF16),
            pltpu.VMEM(own_orbitals.shape, BF16),
            pltpu.SemaphoreType.DMA((2,)),
        ],
        cost_estimate=pl.CostEstimate(
            flops=600_000_000, bytes_accessed=3_000_000, transcendentals=0
        ),
        compiler_params=LIMIT,
        name="early",
    )(lists, counts, own_orbitals, resident_orbitals, right, left)

    def branch(slots):
        def run(own_orbitals, resident_orbitals, received, lists, counts, early, kernel, codes, right, left):
            sent = pl.pallas_call(
                functools.partial(late_kernel, slots),
                out_shape=coded(slots, OUT_SHARE),
                in_specs=[SMEM, SMEM, VMEM, VMEM, VMEM, VMEM, VMEM, VMEM],
                out_specs=VMEM,
                scratch_shapes=[pltpu.VMEM((2, planes, length, length), F32), table],
                compiler_params=LIMIT,
                name="late",
            )(lists, counts, own_orbitals, received, early, codes, right, left)
            got = lax.all_to_all(sent, "grid", split_axis=0, concat_axis=0, tiled=True)
            sent = pl.pallas_call(
                functools.partial(middle_kernel, slots, planes),
                out_shape=coded(slots, BACK_SHARE),
                in_specs=[VMEM, VMEM, VMEM],
                out_specs=VMEM,
                scratch_shapes=[pltpu.VMEM((slots, length * rows, length), F32)] * 2 + [table],
                compiler_params=LIMIT,
                name="middle",
            )(got, kernel, left)
            got = lax.all_to_all(sent, "grid", split_axis=0, concat_axis=0, tiled=True)
            return pl.pallas_call(
                functools.partial(final_kernel, slots),
                out_shape=(
                    jax.ShapeDtypeStruct(own_orbitals.shape, BF16),
                    jax.ShapeDtypeStruct((pieces, bands, bands, length), F32),
                ),
                in_specs=[SMEM, SMEM, VMEM, VMEM, VMEM, VMEM, VMEM, VMEM],
                out_specs=(ANY, VMEM),
                scratch_shapes=[
                    pltpu.VMEM((slots, length, length), F32),
                    pltpu.VMEM((bands * bands, 8, length), F32),
                    pltpu.VMEM(own_orbitals.shape, BF16),
                    pltpu.SemaphoreType.DMA((planes // 2, bands)),
                ],
                compiler_params=LIMIT,
                name="final",
            )(lists, counts, own_orbitals, resident_orbitals, received, got, right, left)

        return run

    exchange, terms = lax.switch(
        index[0],
        [branch(2), branch(3), branch(4)],
        own_orbitals,
        resident_orbitals,
        received,
        lists,
        counts,
        early,
        kernel,
        codes,
        right,
        left,
    )
    terms = lax.all_to_all(terms, "grid", split_axis=0, concat_axis=0, tiled=True)
    return exchange, jnp.sum(terms, axis=(0, 3))


def solution(mesh):
    in_specs = (
        P(None, None),
        P(None, None),
        P("band", "grid", None, None),
        P("band", "grid", None, None),
        P("band", None, None, None),
        P("band", None),
    )
    out_specs = (P("band", "grid", None, None), P("band", None))
    mapped = jax.shard_map(
        on_device, mesh=mesh, in_specs=in_specs, out_specs=out_specs, check_vma=False
    )

    def step(own_orbitals, resident_orbitals, pair_lists, pair_counts):
        length = own_orbitals.shape[-1]
        right, left = jnp.asarray(right_table(length)), jnp.asarray(left_table(length))
        return mapped(right, left, own_orbitals, resident_orbitals, pair_lists, pair_counts)

    return step
```

profile of v0, /device:TPU:16, one launch (start us, length us, event | category | flops | bytes accessed | tf_op | source)
XLA Modules:
  0.0 86.4 jit_solution(12721276414005931048)
XLA Ops:
  0.6 0.0 copy-start.1
  0.6 0.0 copy-start.3
  0.7 0.0 copy-start.2
  0.7 0.0 copy-start.5
  0.7 0.0 copy-start.4
  0.7 0.0 copy-start
  0.7 0.1 collective-permute-start
  0.8 3.7 %early.1 = (s16[16,16,8,128]{3,2,1,0:T(8,128)(2,1)S(1)}, f32[128,1024]{1,0:T(8,128)S(1)}, f32[2,128,128]{2,1,0:T(8,128)S(1)}, s32[1]{0:T(128)}) custom-call(s32[1,2,2,2]{3,2,1,0:T(2,128)} %lists_ref.1, s32[1,2]{1,0:T(1,128)} %counts_ref.1, bf16[2,8,128,128]{3,2,1,0:T(8,128)(2,1)} %own_hbm.1, bf16[2,8,128,128]{3,2,1,0:T(8,128)(2,1)} %resident_hbm.1, ...), custom_call_target="tpu_custom_call" | custom-call | flops 600000000 | bytes 3000000 | tf_op jit(solution)/shard_map/early/pallas_call | solution.py:436
  5.2 5.3 %collective-permute-done = bf16[2,8,128,128]{3,2,1,0:T(8,128)(2,1)S(1)} collective-permute-done((bf16[2,8,128,128]{3,2,1,0:T(8,128)(2,1)}, bf16[2,8,128,128]{3,2,1,0:T(8,128)(2,1)S(1)}, u32[]{:S(2)}, u32[]{:S(2)}) %collective-permute-start) | collective-permute-done | bytes 524320 | tf_op jit(solution)/shard_map/ppermute | solution.py:25
  10.5 0.0 copy-done.1
  10.5 0.0 copy-done.3
  10.5 0.0 copy-done.2
  10.5 0.0 copy-done.5
  10.5 0.0 copy-done.4
  10.5 0.0 copy-done
  10.5 62.0 %conditional.1 = ((bf16[2,8,128,128]{3,2,1,0:T(8,128)(2,1)}, f32[16,2,2,128]{3,2,1,0:T(2,128)S(1)})) conditional(s32[]{:T(128)} %bitcast, (s32[1,2,2,2]{3,2,1,0:T(2,128)S(1)}, s32[1,2]{1,0:T(1,128)S(1)}, bf16[2,8,128,128]{3,2,1,0:T(8,128)(2,1)S(1)}, bf16[2,8,128,128]{3,2,1,0:T(8,128)(2,1)S(1)}, ...), branch_computations={%region_0.0_spmd, %region_1.0_spmd, %region_2.0_spmd} | conditional | bytes 4390920 | solution.py:501
  10.5 1.5 %late.3 = s16[16,17,8,128]{3,2,1,0:T(8,128)(2,1)S(1)} custom-call(s32[1,2,2,2]{3,2,1,0:T(2,128)S(1)} %get-tuple-element.60.lists_ref, s32[1,2]{1,0:T(1,128)S(1)} %get-tuple-element.61.counts_ref, bf16[2,8,128,128]{3,2,1,0:T(8,128)(2,1)S(1)} %get-tuple-element.62.own_ref, bf16[2,8,128,128]{3,2,1,0:T(8,128)(2,1)S(1)} %get-tuple-element.64.received_ref, ...), custom_call_target="tpu_custom_call" | custom-call | tf_op jit(solution)/shard_map/cond/branch_0_fun/late/pallas_call | solution.py:461
  12.0 32.7 %all_to_all.29.got_ref = s16[16,17,8,128]{3,2,1,0:T(8,128)(2,1)S(1)} all-to-all(s16[16,17,8,128]{3,2,1,0:T(8,128)(2,1)S(1)} %late.3), channel_id=1, replica_groups=mesh['band'=16,'grid'=16] {'grid'}, dimensions={0} | all-to-all | bytes 1114112 | tf_op jit(solution)/shard_map/cond/branch_0_fun/all_to_all | solution.py:470
  44.7 1.3 %middle.3 = s16[16,17,8,128]{3,2,1,0:T(8,128)(2,1)S(1)} custom-call(s16[16,17,8,128]{3,2,1,0:T(8,128)(2,1)S(1)} %all_to_all.29.got_ref, f32[128,1024]{1,0:T(8,128)S(1)} %get-tuple-element.69.kernel_ref, bf16[256,256]{1,0:T(8,128)(2,1)S(1)} %get-tuple-element.68.left_ref), custom_call_target="tpu_custom_call" | custom-call | tf_op jit(solution)/shard_map/cond/branch_0_fun/middle/pallas_call | solution.py:471
  46.0 23.9 %all_to_all.30.got_ref = s16[16,17,8,128]{3,2,1,0:T(8,128)(2,1)S(1)} all-to-all(s16[16,17,8,128]{3,2,1,0:T(8,128)(2,1)S(1)} %middle.3), channel_id=1, replica_groups=mesh['band'=16,'grid'=16] {'grid'}, dimensions={0} | all-to-all | bytes 1114112 | tf_op jit(solution)/shard_map/cond/branch_0_fun/all_to_all | solution.py:480
  69.9 2.4 %final.3 = (bf16[2,8,128,128]{3,2,1,0:T(8,128)(2,1)}, f32[16,2,2,128]{3,2,1,0:T(2,128)S(1)}) custom-call(s32[1,2,2,2]{3,2,1,0:T(2,128)S(1)} %get-tuple-element.60.lists_ref, s32[1,2]{1,0:T(1,128)S(1)} %get-tuple-element.61.counts_ref, bf16[2,8,128,128]{3,2,1,0:T(8,128)(2,1)S(1)} %get-tuple-element.62.own_ref, ...), custom_call_target="tpu_custom_call" | custom-call | tf_op jit(solution)/shard_map/cond/branch_0_fun/final/pallas_call | solution.py:481
  72.6 13.1 %all_to_all.35 = f32[16,2,2,128]{3,2,1,0:T(2,128)S(1)} all-to-all(f32[16,2,2,128]{3,2,1,0:T(2,128)S(1)} %get-tuple-element.103), channel_id=1, replica_groups=mesh['band'=16,'grid'=16] {'grid'}, dimensions={0} | all-to-all | bytes 65536 | tf_op jit(solution)/shard_map/all_to_all | solution.py:515
  85.7 0.7 reduce_sum.9
Async XLA Ops:
  0.6 9.9 %copy-start.1 = (bf16[256,256]{1,0:T(8,128)(2,1)S(1)}, bf16[256,256]{1,0:T(8,128)(2,1)}, u32[]{:S(2)}) copy-start(bf16[256,256]{1,0:T(8,128)(2,1)} %constant.13.clone.left_ref) | copy-start | bytes 393220
  0.6 9.9 %copy-start.3 = (bf16[256,256]{1,0:T(8,128)(2,1)S(1)}, bf16[256,256]{1,0:T(8,128)(2,1)}, u32[]{:S(2)}) copy-start(bf16[256,256]{1,0:T(8,128)(2,1)} %constant.12.clone.right_ref) | copy-start | bytes 393220
  0.7 9.8 %copy-start.2 = (bf16[2,8,128,128]{3,2,1,0:T(8,128)(2,1)S(1)}, bf16[2,8,128,128]{3,2,1,0:T(8,128)(2,1)}, u32[]{:S(2)}) copy-start(bf16[2,8,128,128]{3,2,1,0:T(8,128)(2,1)} %resident_hbm.1) | copy-start | bytes 1572868
  0.7 9.8 %copy-start.5 = (s32[1,2]{1,0:T(1,128)S(1)}, s32[1,2]{1,0:T(1,128)}, u32[]{:S(2)}) copy-start(s32[1,2]{1,0:T(1,128)} %counts_ref.1) | copy-start | bytes 28
  0.7 9.8 %copy-start.4 = (s32[1,2,2,2]{3,2,1,0:T(2,128)S(1)}, s32[1,2,2,2]{3,2,1,0:T(2,128)}, u32[]{:S(2)}) copy-start(s32[1,2,2,2]{3,2,1,0:T(2,128)} %lists_ref.1) | copy-start | bytes 100
  0.7 9.8 %copy-start = (bf16[2,8,128,128]{3,2,1,0:T(8,128)(2,1)S(1)}, bf16[2,8,128,128]{3,2,1,0:T(8,128)(2,1)}, u32[]{:S(2)}) copy-start(bf16[2,8,128,128]{3,2,1,0:T(8,128)(2,1)} %own_hbm.1) | copy-start | bytes 1572868
  0.7 9.8 %collective-permute-start = (bf16[2,8,128,128]{3,2,1,0:T(8,128)(2,1)}, bf16[2,8,128,128]{3,2,1,0:T(8,128)(2,1)S(1)}, u32[]{:S(2)}, u32[]{:S(2)}) collective-permute-start(bf16[2,8,128,128]{3,2,1,0:T(8,128)(2,1)} %resident_hbm.1), channel_id=1, source_target_pairs={{0,16},{16,32},{32,48},{48,64},{64,80},{80,96},{96,112},{112,128},... | collective-permute-start | bytes 1572872 | tf_op jit(solution)/shard_map/ppermute | solution.py:25
where the time goes:
time: 86.8 us; the launch traced here: 86.4 us
  blocking collectives  69.8 us (80%)
  Pallas kernels  8.87 us (10%)
  waiting for transfers between devices  5.31 us (6%)
  between operations  1.38 us (2%)
    all_to_all x2, blocking collectives, run(): got = lax.all_to_all(sent, 'grid', split_axis=0, concat_axis=0, tiled=True)  56.6 us
    all_to_all x1, blocking collectives, on_device(): lax.all_to_all(terms, 'grid', split_axis=0, concat_axis=0, tiled=True)  13.1 us
    ppermute x1, waiting for transfers between devices, passed_along(): lax.ppermute(x, axis, [(i, (i + by) % length) for i in range(length)])  5.31 us
    pallas_call x1, Pallas kernels, on_device(): pl.pallas_call(early_kernel, out_shape=(coded(2, 0), jax.ShapeDtypeStruct...  3.74 us
    pallas_call x1, Pallas kernels, run(): pl.pallas_call(functools.partial(final_kernel, slots), out_shape=(jax.Sha...  2.39 us
  transfers between devices with their start and end apart: 1, of which 1 were waited for; matrix products, arithmetic and copies ran while one was open for 0% of the time, Pallas kernels for 4%

commit v1 on v0

--- a/solution.py
+++ b/solution.py
@@ -16,7 +16,7 @@
 FLOOR = 2.0**-110
 GROUP = 4
 OUT_SHARE = 4
-BACK_SHARE = 2
+BACK_SHARE = 4
 LIMIT = pltpu.CompilerParams(vmem_limit_bytes=20 << 20)
 
 

time: 86.8 us -> 86.1 us (level)
  the two profiles are of different devices: /device:TPU:16 before, /device:TPU:10 now
where the time goes in v1:
time: 86.1 us; the launch traced here: 84.5 us
  blocking collectives  68.6 us (80%)
  Pallas kernels  9.03 us (10%)
  waiting for transfers between devices  4.41 us (5%)
  between operations  1.38 us (2%)
    all_to_all x2, blocking collectives, run(): got = lax.all_to_all(sent, 'grid', split_axis=0, concat_axis=0, tiled=True)  55.3 us
    all_to_all x1, blocking collectives, on_device(): lax.all_to_all(terms, 'grid', split_axis=0, concat_axis=0, tiled=True)  13.4 us
    ppermute x1, waiting for transfers between devices, passed_along(): lax.ppermute(x, axis, [(i, (i + by) % length) for i in range(length)])  4.41 us
    pallas_call x1, Pallas kernels, on_device(): pl.pallas_call(early_kernel, out_shape=(coded(2, 0), jax.ShapeDtypeStruct...  3.74 us
    pallas_call x1, Pallas kernels, run(): pl.pallas_call(functools.partial(final_kernel, slots), out_shape=(jax.Sha...  2.48 us
  transfers between devices with their start and end apart: 1, of which 1 were waited for; matrix products, arithmetic and copies ran while one was open for 0% of the time, Pallas kernels for 4%

profile of v1, /device:TPU:10, one launch (start us, length us, event | category | flops | bytes accessed | tf_op | source)
XLA Modules:
  0.0 84.5 jit_solution(13087441003025506407)
XLA Ops:
  0.6 0.0 copy-start.1
  0.6 0.0 copy-start.3
  0.7 0.0 copy-start.2
  0.7 0.0 copy-start.5
  0.7 0.0 copy-start.4
  0.7 0.0 copy-start
  0.7 0.1 collective-permute-start
  0.8 3.7 %early.1 = (s16[16,16,8,128]{3,2,1,0:T(8,128)(2,1)S(1)}, f32[128,1024]{1,0:T(8,128)S(1)}, f32[2,128,128]{2,1,0:T(8,128)S(1)}, s32[1]{0:T(128)}) custom-call(s32[1,2,2,2]{3,2,1,0:T(2,128)} %lists_ref.1, s32[1,2]{1,0:T(1,128)} %counts_ref.1, bf16[2,8,128,128]{3,2,1,0:T(8,128)(2,1)} %own_hbm.1, bf16[2,8,128,128]{3,2,1,0:T(8,128)(2,1)} %resident_hbm.1, ...), custom_call_target="tpu_custom_call" | custom-call | flops 600000000 | bytes 3000000 | tf_op jit(solution)/shard_map/early/pallas_call | solution.py:436
  5.2 4.4 %collective-permute-done = bf16[2,8,128,128]{3,2,1,0:T(8,128)(2,1)S(1)} collective-permute-done((bf16[2,8,128,128]{3,2,1,0:T(8,128)(2,1)}, bf16[2,8,128,128]{3,2,1,0:T(8,128)(2,1)S(1)}, u32[]{:S(2)}, u32[]{:S(2)}) %collective-permute-start) | collective-permute-done | bytes 524320 | tf_op jit(solution)/shard_map/ppermute | solution.py:25
  9.6 0.0 copy-done.1
  9.6 0.0 copy-done.3
  9.6 0.0 copy-done.2
  9.6 0.0 copy-done.5
  9.6 0.0 copy-done.4
  9.6 0.0 copy-done
  9.6 60.8 %conditional.1 = ((bf16[2,8,128,128]{3,2,1,0:T(8,128)(2,1)}, f32[16,2,2,128]{3,2,1,0:T(2,128)S(1)})) conditional(s32[]{:T(128)} %bitcast, (s32[1,2,2,2]{3,2,1,0:T(2,128)S(1)}, s32[1,2]{1,0:T(1,128)S(1)}, bf16[2,8,128,128]{3,2,1,0:T(8,128)(2,1)S(1)}, bf16[2,8,128,128]{3,2,1,0:T(8,128)(2,1)S(1)}, ...), branch_computations={%region_0.0_spmd, %region_1.0_spmd, %region_2.0_spmd} | conditional | bytes 4325384 | solution.py:501
  9.6 1.5 %late.3 = s16[16,17,8,128]{3,2,1,0:T(8,128)(2,1)S(1)} custom-call(s32[1,2,2,2]{3,2,1,0:T(2,128)S(1)} %get-tuple-element.60.lists_ref, s32[1,2]{1,0:T(1,128)S(1)} %get-tuple-element.61.counts_ref, bf16[2,8,128,128]{3,2,1,0:T(8,128)(2,1)S(1)} %get-tuple-element.62.own_ref, bf16[2,8,128,128]{3,2,1,0:T(8,128)(2,1)S(1)} %get-tuple-element.64.received_ref, ...), custom_call_target="tpu_custom_call" | custom-call | tf_op jit(solution)/shard_map/cond/branch_0_fun/late/pallas_call | solution.py:461
  11.1 31.3 %all_to_all.29.got_ref = s16[16,17,8,128]{3,2,1,0:T(8,128)(2,1)S(1)} all-to-all(s16[16,17,8,128]{3,2,1,0:T(8,128)(2,1)S(1)} %late.3), channel_id=1, replica_groups=mesh['band'=16,'grid'=16] {'grid'}, dimensions={0} | all-to-all | bytes 1114112 | tf_op jit(solution)/shard_map/cond/branch_0_fun/all_to_all | solution.py:470
  42.4 1.4 %middle.3 = s16[16,17,8,128]{3,2,1,0:T(8,128)(2,1)S(1)} custom-call(s16[16,17,8,128]{3,2,1,0:T(8,128)(2,1)S(1)} %all_to_all.29.got_ref, f32[128,1024]{1,0:T(8,128)S(1)} %get-tuple-element.69.kernel_ref, bf16[256,256]{1,0:T(8,128)(2,1)S(1)} %get-tuple-element.68.left_ref), custom_call_target="tpu_custom_call" | custom-call | tf_op jit(solution)/shard_map/cond/branch_0_fun/middle/pallas_call | solution.py:471
  43.8 23.9 %all_to_all.30.got_ref = s16[16,17,8,128]{3,2,1,0:T(8,128)(2,1)S(1)} all-to-all(s16[16,17,8,128]{3,2,1,0:T(8,128)(2,1)S(1)} %middle.3), channel_id=1, replica_groups=mesh['band'=16,'grid'=16] {'grid'}, dimensions={0} | all-to-all | bytes 1114112 | tf_op jit(solution)/shard_map/cond/branch_0_fun/all_to_all | solution.py:480
  67.7 2.5 %final.3 = (bf16[2,8,128,128]{3,2,1,0:T(8,128)(2,1)}, f32[16,2,2,128]{3,2,1,0:T(2,128)S(1)}) custom-call(s32[1,2,2,2]{3,2,1,0:T(2,128)S(1)} %get-tuple-element.60.lists_ref, s32[1,2]{1,0:T(1,128)S(1)} %get-tuple-element.61.counts_ref, bf16[2,8,128,128]{3,2,1,0:T(8,128)(2,1)S(1)} %get-tuple-element.62.own_ref, ...), custom_call_target="tpu_custom_call" | custom-call | tf_op jit(solution)/shard_map/cond/branch_0_fun/final/pallas_call | solution.py:481
  70.5 13.4 %all_to_all.35 = f32[16,2,2,128]{3,2,1,0:T(2,128)S(1)} all-to-all(f32[16,2,2,128]{3,2,1,0:T(2,128)S(1)} %get-tuple-element.103), channel_id=1, replica_groups=mesh['band'=16,'grid'=16] {'grid'}, dimensions={0} | all-to-all | bytes 65536 | tf_op jit(solution)/shard_map/all_to_all | solution.py:515
  83.8 0.7 reduce_sum.9
Async XLA Ops:
  0.6 9.0 %copy-start.1 = (bf16[256,256]{1,0:T(8,128)(2,1)S(1)}, bf16[256,256]{1,0:T(8,128)(2,1)}, u32[]{:S(2)}) copy-start(bf16[256,256]{1,0:T(8,128)(2,1)} %constant.13.clone.left_ref) | copy-start | bytes 393220
  0.6 9.0 %copy-start.3 = (bf16[256,256]{1,0:T(8,128)(2,1)S(1)}, bf16[256,256]{1,0:T(8,128)(2,1)}, u32[]{:S(2)}) copy-start(bf16[256,256]{1,0:T(8,128)(2,1)} %constant.12.clone.right_ref) | copy-start | bytes 393220
  0.7 8.9 %copy-start.2 = (bf16[2,8,128,128]{3,2,1,0:T(8,128)(2,1)S(1)}, bf16[2,8,128,128]{3,2,1,0:T(8,128)(2,1)}, u32[]{:S(2)}) copy-start(bf16[2,8,128,128]{3,2,1,0:T(8,128)(2,1)} %resident_hbm.1) | copy-start | bytes 1572868
  0.7 8.9 %copy-start.5 = (s32[1,2]{1,0:T(1,128)S(1)}, s32[1,2]{1,0:T(1,128)}, u32[]{:S(2)}) copy-start(s32[1,2]{1,0:T(1,128)} %counts_ref.1) | copy-start | bytes 28
  0.7 8.9 %copy-start.4 = (s32[1,2,2,2]{3,2,1,0:T(2,128)S(1)}, s32[1,2,2,2]{3,2,1,0:T(2,128)}, u32[]{:S(2)}) copy-start(s32[1,2,2,2]{3,2,1,0:T(2,128)} %lists_ref.1) | copy-start | bytes 100
  0.7 8.9 %copy-start = (bf16[2,8,128,128]{3,2,1,0:T(8,128)(2,1)S(1)}, bf16[2,8,128,128]{3,2,1,0:T(8,128)(2,1)}, u32[]{:S(2)}) copy-start(bf16[2,8,128,128]{3,2,1,0:T(8,128)(2,1)} %own_hbm.1) | copy-start | bytes 1572868
  0.7 8.9 %collective-permute-start = (bf16[2,8,128,128]{3,2,1,0:T(8,128)(2,1)}, bf16[2,8,128,128]{3,2,1,0:T(8,128)(2,1)S(1)}, u32[]{:S(2)}, u32[]{:S(2)}) collective-permute-start(bf16[2,8,128,128]{3,2,1,0:T(8,128)(2,1)} %resident_hbm.1), channel_id=1, source_target_pairs={{0,16},{16,32},{32,48},{48,64},{64,80},{80,96},{96,112},{112,128},... | collective-permute-start | bytes 1572872 | tf_op jit(solution)/shard_map/ppermute | solution.py:25
